TPU v7x, 256 devices: a whole 4x4x8 slice. The times are simulated.
256 devices in a mesh: shards: 16 (over x, y), tensor: 4 (over z_hi, core), replica: 4 (over z_lo).
Axes of the slice: x: 4, y: 4, z: 8 (z_hi: 2, z_lo: 4; z = z_hi * 4 + z_lo), core: 2. Of those that a mesh axis runs over, the one named last changes fastest.
Arguments:
- activations: bfloat16 [262144, 1024], P(('shards', 'tensor', 'replica')), may hold values from -24 to 24
- grads_out: bfloat16 [262144, 1024], P(('shards', 'tensor', 'replica')), may hold values from -24 to 24
- grad_parts: float32 [64, 1024, 1024], P(('shards', 'replica'), None, 'tensor'), may hold values from -80 to 80
- old_factors: float32 [16, 128, 128], replicated, may hold values from -16 to 16, as said below
- block_owner: int32 [16], replicated, may hold values from 0 to 15, as said below
- weights: float32 [1024, 1024], P(('shards', 'replica'), 'tensor'), may hold values from -0.1875 to 0.1875
- momentum: float32 [1024, 1024], P(('shards', 'replica'), 'tensor'), may hold values from -4 to 4
Outputs:
- weights_next: float32 [1024, 1024], P(None, 'tensor')
- momentum_next: float32 [1024, 1024], P(('shards', 'replica'), 'tensor')
- next_factor_blocks: float32 [32, 128, 128], P('shards')
Inputs may be any that keep to these rules, and one draw needn't show every extreme that they name: `block_owner`: each shard index owns at most 2 of the 16 blocks, and some index owns exactly 2. `old_factors`: each block is symmetric and positive definite.
All inputs are finite; a program needn't handle non-finite values. Where the computation divides by a largest or mean magnitude, that divisor is 1e-20 or more.
Results may differ from a plain program's by a relative error of at most 0.0003.
Values sent between devices are 32-bit elements; how exact they have to be, the bound alone decides.
No kernel may reach another device: no remote copies, remote signals or barrier semaphores. Data moves between devices by JAX's collectives and lax.ppermute only.
A program may use at most 64 MiB of HBM per device.

v0:
```python
import jax
import jax.numpy as jnp
from jax import lax
from jax.sharding import PartitionSpec as P

NS_STEPS = 4
exact_mode = lax.Precision.HIGHEST
decay_rate = 0.75
damping = 0.1
damp_shift = 0.001
clip_norm = 256.0
momentum_rate = 0.9
step_rate = 0.05


def sample_stats(samples, block_size):
    sample_rows, width = samples.shape
    blocks = samples.reshape(sample_rows, width // block_size, block_size)
    return jnp.einsum("tnb,tnc->nbc", blocks, blocks, preferred_element_type=jnp.float32)


def newton_inverse(mixed_factor_blocks):
    block_size = mixed_factor_blocks.shape[-1]
    identity = jnp.eye(block_size, dtype=jnp.float32)
    traces = jnp.trace(mixed_factor_blocks, axis1=1, axis2=2)
    damped = (
        mixed_factor_blocks + (damping * traces / block_size + damp_shift)[:, None, None] * identity
    )
    bounds = jnp.max(jnp.sum(jnp.abs(damped), axis=2), axis=1)
    approx = identity[None, :, :] / bounds[:, None, None]
    for iteration in range(NS_STEPS):
        left_part = jnp.einsum("nab,nbc->nac", approx, damped, precision=exact_mode)
        approx = 2.0 * approx - jnp.einsum("nab,nbc->nac", left_part, approx, precision=exact_mode)
    return approx


def swap(value, axis, flip):
    size = lax.axis_size(axis)
    return lax.ppermute(value, axis, [(i, i ^ flip) for i in range(size)])


def exchange_sum(value, axis):
    parts = [swap(value, axis, flip) for flip in range(1, lax.axis_size(axis))]
    for part in parts:
        value = value + part
    return value


def body(activations, grads_out, grad_parts, old_factors, block_owner, weights, momentum):
    shard_count = lax.axis_size("shards")
    block_count = old_factors.shape[0]
    block_size = old_factors.shape[1]
    capacity = (block_count + shard_count - 1) // shard_count + 1
    sample_count = (
        activations.shape[0] * shard_count * lax.axis_size("tensor") * lax.axis_size("replica")
    )
    partial_grad = grad_parts[0]
    row_count, col_count = partial_grad.shape
    left_count = row_count // block_size
    right_count = col_count // block_size
    base = weights - step_rate * momentum_rate * momentum
    base = lax.all_gather(base, "replica", axis=0, tiled=True)
    base = lax.all_gather(base, "shards", axis=0, tiled=True)
    stats = jnp.concatenate(
        [sample_stats(activations, block_size), sample_stats(grads_out, block_size)], axis=0
    )
    piece_rows = row_count // shard_count
    grad_pieces = [
        partial_grad[:, n * block_size : (n + 1) * block_size].reshape(
            shard_count, piece_rows, block_size
        )
        for n in range(right_count)
    ]
    outgoing = jnp.concatenate([stats] + grad_pieces, axis=1)
    incoming = lax.all_to_all(outgoing, "shards", 0, 0)
    summed = exchange_sum(jnp.sum(incoming, axis=0), "replica")
    own_stats = summed[:block_size]
    own_stats = own_stats + swap(own_stats, "tensor", 1)
    own_stats = own_stats + swap(own_stats, "tensor", 2)
    own = jnp.concatenate([own_stats, summed[block_size:]], axis=0)
    own, base = lax.optimization_barrier((own, base))
    gathered = lax.all_to_all(
        jnp.broadcast_to(own[None], (shard_count,) + own.shape), "shards", 0, 0
    )
    blended = decay_rate * old_factors + (1.0 - decay_rate) * (
        gathered[:, :block_size] / sample_count
    )
    grad_columns = [
        gathered[:, block_size + n * piece_rows : block_size + (n + 1) * piece_rows].reshape(
            left_count, block_size, block_size
        )
        for n in range(right_count)
    ]
    positions = jnp.arange(block_count, dtype=jnp.int32)
    earlier = (block_owner[:, None] == block_owner[None, :]) & (
        positions[None, :] < positions[:, None]
    )
    slots = block_owner * capacity + jnp.sum(earlier.astype(jnp.int32), axis=1)
    owned = []
    for place in range(capacity):
        match = slots == lax.axis_index("shards") * capacity + place
        which = jnp.sum(jnp.where(match, positions, 0))
        block = lax.dynamic_index_in_dim(blended, which, 0, keepdims=False)
        owned.append(jnp.where(jnp.any(match), block, 0.0))
    owned_blocks = jnp.stack(owned)
    right_first = left_count + lax.axis_index("tensor") * right_count
    needed = jnp.concatenate(
        [blended[:left_count], lax.dynamic_slice_in_dim(blended, right_first, right_count, 0)],
        axis=0,
    )
    inverses = newton_inverse(needed)
    precond_columns = []
    for n in range(right_count):
        left_part = jnp.einsum(
            "nab,nbc->nac", inverses[:left_count], grad_columns[n], precision=exact_mode
        )
        precond_columns.append(
            jnp.einsum("nab,bc->nac", left_part, inverses[left_count + n], precision=exact_mode)
        )
    local_sum = sum((jnp.sum(p * g) for p, g in zip(precond_columns, grad_columns)))
    precond = jnp.concatenate([p.reshape(row_count, block_size) for p in precond_columns], axis=1)
    alignment_sum = lax.psum(local_sum, "tensor")
    clip_scale = jnp.minimum(1.0, clip_norm / jnp.sqrt(alignment_sum))
    own_rows = weights.shape[0]
    first_row = lax.axis_index(("shards", "replica")) * own_rows
    own_precond = lax.dynamic_slice_in_dim(precond, first_row, own_rows, 0)
    momentum_next = momentum_rate * momentum + clip_scale * own_precond
    weights_next = base - step_rate * clip_scale * precond
    return (weights_next, momentum_next, owned_blocks)


def solution(mesh):
    placed = (
        P(("shards", "tensor", "replica"), None),
        P(("shards", "tensor", "replica"), None),
        P(("shards", "replica"), None, "tensor"),
        P(),
        P(),
        P(("shards", "replica"), "tensor"),
        P(("shards", "replica"), "tensor"),
    )
    return jax.shard_map(
        body,
        mesh=mesh,
        in_specs=placed,
        out_specs=(P(None, "tensor"), P(("shards", "replica"), "tensor"), P("shards", None, None)),
        check_vma=False,
    )
```

profile of v0, /device:TPU:1, one launch (start us, length us, event | category | flops | bytes accessed | tf_op | source)
XLA Modules:
  0.0 160.7 jit_solution(14424945549130774064)
XLA Ops:
  7.2 0.0 copy-start
  7.2 0.0 copy-start.7
  7.2 1.6 copy-done
  8.8 1.1 fusion.3
  9.8 0.0 copy-done.7
  9.8 0.0 copy-start.3
  9.8 1.1 fusion
  11.0 0.1 copy-done.3
  11.1 0.1 fusion.27
  11.1 1.5 pad_maximum_fusion
  12.6 0.0 copy-start.4
  12.6 0.0 copy-start.5
  12.6 7.8 %all-to-all-start = ((f32[16,256,128]{2,1,0:T(8,128)}), f32[16,256,128]{2,1,0:T(8,128)}, u32[]{:S(2)}, u32[]{:S(2)}) async-start(f32[16,256,128]{2,1,0:T(8,128)} %pad_maximum_fusion), calls=%async_computation | async-start | bytes 4194304 | tf_op jit(solution)/shard_map/all_to_all | solution.py:75
  20.4 0.0 all-gather.2.cloned.1.call-start
  20.4 0.0 copy-done.4
  20.4 0.0 copy-done.5
  20.5 13.0 %all_gather.6 = f32[64,256]{1,0:T(8,128)} all-gather(f32[16,256]{1,0:T(8,128)S(1)} %multiply_subtract_fusion), channel_id=1, replica_groups=mesh['shards'=16,'tensor'=4,'replica'=4] {'replica'}, dimensions={0}, use_global_device_ids=true | all-gather | bytes 81920 | tf_op jit(solution)/shard_map/all_gather | solution.py:62
  33.4 0.0 all-gather.2.cloned.1.call-update
  33.4 14.8 %all-to-all-done = f32[16,256,128]{2,1,0:T(8,128)} async-done(((f32[16,256,128]{2,1,0:T(8,128)}), f32[16,256,128]{2,1,0:T(8,128)}, u32[]{:S(2)}, u32[]{:S(2)}) %all-to-all-start) | async-done | bytes 2097184 | tf_op jit(solution)/shard_map/all_to_all | solution.py:75
  48.3 1.7 %reduce_sum.73 = f32[256,128]{1,0:T(8,128)S(1)} reduce(f32[16,256,128]{2,1,0:T(8,128)} %all-to-all-done, f32[]{:T(128)} %constant.25.clone.1), dimensions={0}, to_apply=%region_0.0 | reduce | flops 491520 | bytes 2228228 | tf_op jit(solution)/shard_map/reduce_sum | solution.py:76
  50.0 4.5 %collective-permute-start.2 = (f32[256,128]{1,0:T(8,128)S(1)}, f32[256,128]{1,0:T(8,128)S(1)}, u32[]{:S(2)}, u32[]{:S(2)}) collective-permute-start(f32[256,128]{1,0:T(8,128)S(1)} %reduce_sum.73), channel_id=1, source_target_pairs={{0,3},{1,2},{2,1},{3,0},{4,7},{5,6},{6,5},{7,4},{8,11},{9,10},{10,... | collective-permute-start | bytes 393224 | tf_op jit(solution)/shard_map/ppermute | solution.py:39
  54.5 0.0 collective-permute-start.1
  54.5 0.4 collective-permute-start
  54.8 2.0 %collective-permute-done.2 = f32[256,128]{1,0:T(8,128)S(1)} collective-permute-done((f32[256,128]{1,0:T(8,128)S(1)}, f32[256,128]{1,0:T(8,128)S(1)}, u32[]{:S(2)}, u32[]{:S(2)}) %collective-permute-start.2) | collective-permute-done | bytes 131104 | tf_op jit(solution)/shard_map/ppermute | solution.py:39
  56.9 7.0 %collective-permute-done.1 = f32[256,128]{1,0:T(8,128)S(1)} collective-permute-done((f32[256,128]{1,0:T(8,128)S(1)}, f32[256,128]{1,0:T(8,128)S(1)}, u32[]{:S(2)}, u32[]{:S(2)}) %collective-permute-start.1) | collective-permute-done | bytes 131104 | tf_op jit(solution)/shard_map/ppermute | solution.py:39
  63.9 0.0 collective-permute-done
  64.0 2.2 %collective-permute-start.3 = (f32[128,128]{1,0:T(8,128)S(1)}, f32[128,128]{1,0:T(8,128)S(1)}, u32[]{:S(2)}, u32[]{:S(2)}) collective-permute-start(f32[128,128]{1,0:T(8,128)S(1)} %slice.47), channel_id=1, source_target_pairs={{0,4},{4,0},{8,12},{12,8},{1,5},{5,1},{9,13},{13,9},{2,6},{6,2},{1... | collective-permute-start | bytes 196616 | tf_op jit(solution)/shard_map/ppermute | solution.py:39
  66.1 0.9 collective-permute-done.3
  67.1 5.9 %collective-permute-start.4 = (f32[128,128]{1,0:T(8,128)S(1)}, f32[128,128]{1,0:T(8,128)S(1)}, u32[]{:S(2)}, u32[]{:S(2)}) collective-permute-start(f32[128,128]{1,0:T(8,128)S(1)} %get-tuple-element.18), channel_id=1, source_target_pairs={{0,8},{4,12},{8,0},{12,4},{1,9},{5,13},{9,1},{13,5},{2,10},{6,14},... | collective-permute-start | bytes 196616 | tf_op jit(solution)/shard_map/ppermute | solution.py:39
  73.0 2.2 %collective-permute-done.4 = f32[128,128]{1,0:T(8,128)S(1)} collective-permute-done((f32[128,128]{1,0:T(8,128)S(1)}, f32[128,128]{1,0:T(8,128)S(1)}, u32[]{:S(2)}, u32[]{:S(2)}) %collective-permute-start.4) | collective-permute-done | bytes 65568 | tf_op jit(solution)/shard_map/ppermute | solution.py:39
  75.2 9.0 %all-gather.2.cloned.1.call-done = f32[1024,256]{1,0:T(8,128)} async-done(((f32[64,256]{1,0:T(8,128)}), f32[1024,256]{1,0:T(8,128)}) %all-gather.2.cloned.1.call-update) | async-done | bytes 1048592 | tf_op jit(solution)/shard_map/all_gather | solution.py:63
  84.2 1.5 broadcast_in_dim.33
  85.7 5.2 %all-to-all-start.1 = ((f32[16,256,128]{2,1,0:T(8,128)}), f32[16,256,128]{2,1,0:T(8,128)}, u32[]{:S(2)}, u32[]{:S(2)}) async-start(f32[16,256,128]{2,1,0:T(8,128)} %broadcast_in_dim.33), calls=%async_computation.1 | async-start | bytes 4194304 | tf_op jit(solution)/shard_map/all_to_all | solution.py:82
  90.9 0.0 copy-done.6
  90.9 0.2 convert_reduce_fusion
  91.0 0.7 compare_reduce_fusion.1
  91.8 0.7 fusion.21
  95.8 20.6 %all-to-all-done.1 = f32[16,256,128]{2,1,0:T(8,128)} async-done(((f32[16,256,128]{2,1,0:T(8,128)}), f32[16,256,128]{2,1,0:T(8,128)}, u32[]{:S(2)}, u32[]{:S(2)}) %all-to-all-start.1) | async-done | bytes 2097184 | tf_op jit(solution)/shard_map/all_to_all | solution.py:82
  116.5 0.0 copy-done.2
  116.5 1.4 fusion.8
  117.8 0.0 copy-start.1
  117.9 0.9 copy-done.1
  118.8 0.2 select_reduce_fusion
  119.0 0.3 abs_reduce_fusion
  119.3 0.1 reduce_max.9
  119.4 0.9 fusion.9
  120.3 0.8 convolution_subtract_fusion.3
  121.2 0.8 fusion.25
  122.0 0.8 convolution_subtract_fusion.2
  122.8 0.8 fusion.24
  123.6 0.8 convolution_subtract_fusion.1
  124.4 0.8 fusion.23
  125.3 0.8 convolution_subtract_fusion
  126.1 1.3 fusion.26
  127.4 0.6 fusion.28
  128.0 0.6 fusion.17
  128.6 0.6 fusion.29
  129.3 0.6 fusion.16
  129.9 0.8 multiply_reduce_fusion
  132.7 14.8 %psum.7 = f32[]{:T(128)} all-reduce(f32[]{:T(128)S(6)} %add.69), channel_id=1, replica_groups=mesh['shards'=16,'tensor'=4,'replica'=4] {'tensor'}, use_global_device_ids=true, to_apply=%region_6.7 | all-reduce | flops 1 | bytes 8 | tf_op jit(solution)/shard_map/psum | solution.py:122
  148.1 2.1 %dynamic-slice_select_fusion.1 = (f32[1,128,128]{2,1,0:T(8,128)S(1)}, f32[1,128,128]{2,1,0:T(8,128)S(1)}) fusion(f32[16,128,128]{2,1,0:T(8,128)} %copy-done.1, s32[]{:T(128)S(6)} %select_n.46, pred[]{:T(512)} %get-tuple-element.7, s32[]{:T(128)S(6)} %select_n.50, pred[]{:T(512)} %get-tuple-element.8), kind=kLoop, calls=%fused_computation.39 | loop fusion | flops 32768 | bytes 262154 | tf_op jit(solution)/shard_map/jit(_where)/select_n | solution.py:104
  150.3 0.7 pad_maximum_fusion.4
  151.0 0.6 multiply_add_fusion.1
  151.6 2.3 %fusion.7 = f32[1024,256]{1,0:T(8,128)} fusion(f32[1024,256]{1,0:T(8,128)} %all-gather.2.cloned.1.call-done, f32[1024,128]{1,0:T(8,128)S(1)} %bitcast.51, f32[1024,128]{1,0:T(8,128)S(1)} %bitcast.49, f32[]{:T(128)S(6)} %mul_shard_map.3), kind=kLoop, calls=%fused_computation.15 | loop fusion | flops 786432 | bytes 3145732 | tf_op jit(solution)/shard_map/sub | solution.py:128
  (13 shorter events, 0.2 us)
Async XLA Ops:
  7.2 1.6 copy-start
  7.2 2.6 %copy-start.7 = (bf16[1024,1024]{1,0:T(8,128)(2,1)S(1)}, bf16[1024,1024]{1,0:T(8,128)(2,1)}, u32[]{:S(2)}) copy-start(bf16[1024,1024]{1,0:T(8,128)(2,1)} %param.8) | copy-start | bytes 6291460
  9.8 1.2 copy-start.3
  12.6 7.8 %copy-start.4 = (f32[16,256]{1,0:T(8,128)S(1)}, f32[16,256]{1,0:T(8,128)}, u32[]{:S(2)}) copy-start(f32[16,256]{1,0:T(8,128)} %param.13) | copy-start | bytes 49156
  12.6 7.8 %copy-start.5 = (f32[16,256]{1,0:T(8,128)S(1)}, f32[16,256]{1,0:T(8,128)}, u32[]{:S(2)}) copy-start(f32[16,256]{1,0:T(8,128)} %param.12) | copy-start | bytes 49156
  12.6 35.7 %all-to-all-start = ((f32[16,256,128]{2,1,0:T(8,128)}), f32[16,256,128]{2,1,0:T(8,128)}, u32[]{:S(2)}, u32[]{:S(2)}) async-start(f32[16,256,128]{2,1,0:T(8,128)} %pad_maximum_fusion), calls=%async_computation | async-start | bytes 4194304 | tf_op jit(solution)/shard_map/all_to_all | solution.py:75
  20.4 63.8 %all-gather.2.cloned.1.call-start = ((), (), s32[]{:S(2)}) async-start(), calls=%async_computation.2 | async-start | bytes 1114112 | tf_op jit(solution)/shard_map/all_gather | solution.py:63
  50.0 6.9 %collective-permute-start.2 = (f32[256,128]{1,0:T(8,128)S(1)}, f32[256,128]{1,0:T(8,128)S(1)}, u32[]{:S(2)}, u32[]{:S(2)}) collective-permute-start(f32[256,128]{1,0:T(8,128)S(1)} %reduce_sum.73), channel_id=1, source_target_pairs={{0,3},{1,2},{2,1},{3,0},{4,7},{5,6},{6,5},{7,4},{8,11},{9,10},{10,... | collective-permute-start | bytes 393224 | tf_op jit(solution)/shard_map/ppermute | solution.py:39
  54.5 9.4 %collective-permute-start.1 = (f32[256,128]{1,0:T(8,128)S(1)}, f32[256,128]{1,0:T(8,128)S(1)}, u32[]{:S(2)}, u32[]{:S(2)}) collective-permute-start(f32[256,128]{1,0:T(8,128)S(1)} %reduce_sum.73), channel_id=1, source_target_pairs={{0,2},{1,3},{2,0},{3,1},{4,6},{5,7},{6,4},{7,5},{8,10},{9,11},{10,... | collective-permute-start | bytes 393224 | tf_op jit(solution)/shard_map/ppermute | solution.py:39
  54.5 9.4 %collective-permute-start = (f32[256,128]{1,0:T(8,128)S(1)}, f32[256,128]{1,0:T(8,128)S(1)}, u32[]{:S(2)}, u32[]{:S(2)}) collective-permute-start(f32[256,128]{1,0:T(8,128)S(1)} %reduce_sum.73), channel_id=1, source_target_pairs={{0,1},{1,0},{2,3},{3,2},{4,5},{5,4},{6,7},{7,6},{8,9},{9,8},{10,11... | collective-permute-start | bytes 393224 | tf_op jit(solution)/shard_map/ppermute | solution.py:39
  64.0 3.1 %collective-permute-start.3 = (f32[128,128]{1,0:T(8,128)S(1)}, f32[128,128]{1,0:T(8,128)S(1)}, u32[]{:S(2)}, u32[]{:S(2)}) collective-permute-start(f32[128,128]{1,0:T(8,128)S(1)} %slice.47), channel_id=1, source_target_pairs={{0,4},{4,0},{8,12},{12,8},{1,5},{5,1},{9,13},{13,9},{2,6},{6,2},{1... | collective-permute-start | bytes 196616 | tf_op jit(solution)/shard_map/ppermute | solution.py:39
  67.1 8.1 %collective-permute-start.4 = (f32[128,128]{1,0:T(8,128)S(1)}, f32[128,128]{1,0:T(8,128)S(1)}, u32[]{:S(2)}, u32[]{:S(2)}) collective-permute-start(f32[128,128]{1,0:T(8,128)S(1)} %get-tuple-element.18), channel_id=1, source_target_pairs={{0,8},{4,12},{8,0},{12,4},{1,9},{5,13},{9,1},{13,5},{2,10},{6,14},... | collective-permute-start | bytes 196616 | tf_op jit(solution)/shard_map/ppermute | solution.py:39
  85.7 5.2 %copy-start.6 = (s32[16]{0:T(128)S(1)}, s32[16]{0:T(128)}, u32[]{:S(2)}) copy-start(s32[16]{0:T(128)} %param.11) | copy-start | bytes 196
  85.7 30.8 %copy-start.2 = (f32[16,128,128]{2,1,0:T(8,128)S(1)}, f32[16,128,128]{2,1,0:T(8,128)}, u32[]{:S(2)}) copy-start(f32[16,128,128]{2,1,0:T(8,128)} %param.10) | copy-start | bytes 3145732
  85.7 30.8 %all-to-all-start.1 = ((f32[16,256,128]{2,1,0:T(8,128)}), f32[16,256,128]{2,1,0:T(8,128)}, u32[]{:S(2)}, u32[]{:S(2)}) async-start(f32[16,256,128]{2,1,0:T(8,128)} %broadcast_in_dim.33), calls=%async_computation.1 | async-start | bytes 4194304 | tf_op jit(solution)/shard_map/all_to_all | solution.py:82
  117.8 1.0 copy-start.1
Sparse Core Ops, SparseCore 0:
  33.6 50.5 all-gather.1
where the time goes:
time: 161 us
  waiting for transfers between devices  56.6 us (35%)
  blocking collectives  27.7 us (17%)
  starting transfers between devices  25.9 us (16%)
  between operations  20.3 us (13%)
  other arithmetic  13.4 us (8%)
  matrix products  11.2 us (7%)
  local copies, waits for them, and re-layouts  5.53 us (3%)
    all_to_all x1, waiting for transfers between devices, body(): lax.all_to_all(jnp.broadcast_to(own[None], (shard_count,) + own.shape), '...  20.6 us
    all_to_all x1, waiting for transfers between devices, body(): incoming = lax.all_to_all(outgoing, 'shards', 0, 0)  14.8 us
    psum x1, blocking collectives, body(): alignment_sum = lax.psum(local_sum, 'tensor')  14.8 us
    ppermute x5, starting transfers between devices, swap(): return lax.ppermute(value, axis, [(i, i ^ flip) for i in range(size)])  13 us
    all_gather x1, blocking collectives, body(): base = lax.all_gather(base, 'replica', axis=0, tiled=True)  13 us
    ppermute x5, waiting for transfers between devices, swap(): return lax.ppermute(value, axis, [(i, i ^ flip) for i in range(size)])  12.1 us
    all_gather x1, waiting for transfers between devices, body(): base = lax.all_gather(base, 'shards', axis=0, tiled=True)  8.98 us
    all_to_all x1, starting transfers between devices, body(): incoming = lax.all_to_all(outgoing, 'shards', 0, 0)  7.77 us
  transfers between devices with their start and end apart: 8, of which 7 were waited for; matrix products, arithmetic and copies ran while one was open for 2% of the time, Pallas kernels for 0%

commit v1 on v0

--- a/solution.py
+++ b/solution.py
@@ -60,7 +60,9 @@
     right_count = col_count // block_size
     base = weights - step_rate * momentum_rate * momentum
     base = lax.all_gather(base, "replica", axis=0, tiled=True)
-    base = lax.all_gather(base, "shards", axis=0, tiled=True)
+    base = jnp.concatenate(
+        lax.all_to_all(jnp.stack([base] * lax.axis_size("shards")), "shards", 0, 0), axis=0
+    )
     stats = jnp.concatenate(
         [sample_stats(activations, block_size), sample_stats(grads_out, block_size)], axis=0
     )

time: 161 us -> 146 us (0.907)
  between operations: 20.3 us -> 6.95 us
  waiting for transfers between devices: 56.6 us -> 49.3 us
  starting transfers between devices: 25.9 us -> 31.2 us
    all_gather x1 -> x0, waiting for transfers between devices: 8.98 us -> none  [body(): base = lax.all_gather(base, 'shards', axis=0, tiled=True)]
    all_to_all x0 -> x1, starting transfers between devices: none -> 3.91 us  [body(): lax.all_to_all(jnp.stack([base] * lax.axis_size('shards')), 'shards', 0, 0)]
    all_to_all x1, starting transfers between devices: 5.17 us -> 6.89 us  [body(): lax.all_to_all(jnp.broadcast_to(own[None], (shard_count,) + own.shape), '...]
  transfers between devices with their start and end apart: 8 -> 8, of which waited for: 7 -> 6; matrix products, arithmetic and copies ran while one was open for 2% -> 2% of each run, Pallas kernels for 0% -> 0%
where the time goes in v1:
time: 146 us
  waiting for transfers between devices  49.3 us (34%)
  starting transfers between devices  31.2 us (21%)
  blocking collectives  26.7 us (18%)
  other arithmetic  13.6 us (9%)
  matrix products  11.2 us (8%)
  between operations  6.95 us (5%)
  local copies, waits for them, and re-layouts  6.74 us (5%)
    all_to_all x1, waiting for transfers between devices, body(): lax.all_to_all(jnp.broadcast_to(own[None], (shard_count,) + own.shape), '...  21.6 us
    all_to_all x1, waiting for transfers between devices, body(): incoming = lax.all_to_all(outgoing, 'shards', 0, 0)  15.2 us
    psum x1, blocking collectives, body(): alignment_sum = lax.psum(local_sum, 'tensor')  14.1 us
    all_gather x1, blocking collectives, body(): base = lax.all_gather(base, 'replica', axis=0, tiled=True)  12.7 us
    ppermute x5, starting transfers between devices, swap(): return lax.ppermute(value, axis, [(i, i ^ flip) for i in range(size)])  12.6 us
    ppermute x5, waiting for transfers between devices, swap(): return lax.ppermute(value, axis, [(i, i ^ flip) for i in range(size)])  12.4 us
    all_to_all x1, starting transfers between devices, body(): incoming = lax.all_to_all(outgoing, 'shards', 0, 0)  7.77 us
    all_to_all x1, starting transfers between devices, body(): lax.all_to_all(jnp.broadcast_to(own[None], (shard_count,) + own.shape), '...  6.89 us
  transfers between devices with their start and end apart: 8, of which 6 were waited for; matrix products, arithmetic and copies ran while one was open for 2% of the time, Pallas kernels for 0%

profile of v1, /device:TPU:1, one launch (start us, length us, event | category | flops | bytes accessed | tf_op | source)
XLA Modules:
  0.0 145.7 jit_solution(14053450389647477167)
XLA Ops:
  0.6 0.0 copy-start
  0.6 0.0 copy-start.7
  0.7 1.6 %copy-done = bf16[1024,1024]{1,0:T(8,128)(2,1)S(1)} copy-done((bf16[1024,1024]{1,0:T(8,128)(2,1)S(1)}, bf16[1024,1024]{1,0:T(8,128)(2,1)}, u32[]{:S(2)}) %copy-start) | copy-done | bytes 2097176
  2.2 1.1 fusion.3
  3.3 0.0 copy-done.7
  3.3 0.0 copy-start.3
  3.3 1.1 fusion
  4.5 0.1 copy-done.3
  4.5 0.1 fusion.27
  4.6 1.5 %pad_maximum_fusion = f32[16,256,128]{2,1,0:T(8,128)} fusion(f32[16,64,128]{2,1,0:T(8,128)S(1)} %bitcast.59, f32[16,64,128]{2,1,0:T(8,128)S(1)} %bitcast.58, f32[8,128,128]{2,1,0:T(8,128)S(1)} %fusion, f32[8,128,128]{2,1,0:T(8,128)S(1)} %fusion.3), kind=kLoop, calls=%fused_computation.6 | loop fusion | flops 1572864 | bytes 4194304 | tf_op jit(solution)/shard_map/concatenate | solution.py:76
  6.1 0.0 copy-start.4
  6.1 7.8 %all-to-all-start = ((f32[16,256,128]{2,1,0:T(8,128)}), f32[16,256,128]{2,1,0:T(8,128)}, u32[]{:S(2)}, u32[]{:S(2)}) async-start(f32[16,256,128]{2,1,0:T(8,128)} %pad_maximum_fusion), calls=%async_computation | async-start | bytes 4194304 | tf_op jit(solution)/shard_map/all_to_all | solution.py:77
  13.8 0.0 copy-done.4
  13.8 0.0 copy-done.5
  13.9 12.7 %all_gather.3 = f32[64,256]{1,0:T(8,128)S(1)} all-gather(f32[16,256]{1,0:T(8,128)S(1)} %multiply_subtract_fusion), channel_id=1, replica_groups=mesh['shards'=16,'tensor'=4,'replica'=4] {'replica'}, dimensions={0}, use_global_device_ids=true | all-gather | bytes 81920 | tf_op jit(solution)/shard_map/all_gather | solution.py:62
  26.5 15.2 %all-to-all-done = f32[16,256,128]{2,1,0:T(8,128)} async-done(((f32[16,256,128]{2,1,0:T(8,128)}), f32[16,256,128]{2,1,0:T(8,128)}, u32[]{:S(2)}, u32[]{:S(2)}) %all-to-all-start) | async-done | bytes 2097184 | tf_op jit(solution)/shard_map/all_to_all | solution.py:77
  41.8 1.1 stack.4
  42.8 3.9 %all-to-all-start.1 = ((f32[16,64,256]{2,1,0:T(8,128)}), f32[16,64,256]{2,1,0:T(8,128)S(1)}, u32[]{:S(2)}, u32[]{:S(2)}) async-start(f32[16,64,256]{2,1,0:T(8,128)} %stack.4), calls=%async_computation.1 | async-start | bytes 2097152 | tf_op jit(solution)/shard_map/all_to_all | solution.py:64
  46.8 1.7 %reduce_sum.73 = f32[256,128]{1,0:T(8,128)S(1)} reduce(f32[16,256,128]{2,1,0:T(8,128)} %all-to-all-done, f32[]{:T(128)} %constant.25.clone.1), dimensions={0}, to_apply=%region_0.0 | reduce | flops 491520 | bytes 2228228 | tf_op jit(solution)/shard_map/reduce_sum | solution.py:78
  48.5 4.4 %collective-permute-start.2 = (f32[256,128]{1,0:T(8,128)S(1)}, f32[256,128]{1,0:T(8,128)S(1)}, u32[]{:S(2)}, u32[]{:S(2)}) collective-permute-start(f32[256,128]{1,0:T(8,128)S(1)} %reduce_sum.73), channel_id=1, source_target_pairs={{0,3},{1,2},{2,1},{3,0},{4,7},{5,6},{6,5},{7,4},{8,11},{9,10},{10,... | collective-permute-start | bytes 393224 | tf_op jit(solution)/shard_map/ppermute | solution.py:39
  52.9 0.0 collective-permute-start.1
  52.9 0.4 collective-permute-start
  53.3 2.3 %collective-permute-done.2 = f32[256,128]{1,0:T(8,128)S(1)} collective-permute-done((f32[256,128]{1,0:T(8,128)S(1)}, f32[256,128]{1,0:T(8,128)S(1)}, u32[]{:S(2)}, u32[]{:S(2)}) %collective-permute-start.2) | collective-permute-done | bytes 131104 | tf_op jit(solution)/shard_map/ppermute | solution.py:39
  55.6 7.1 %collective-permute-done.1 = f32[256,128]{1,0:T(8,128)S(1)} collective-permute-done((f32[256,128]{1,0:T(8,128)S(1)}, f32[256,128]{1,0:T(8,128)S(1)}, u32[]{:S(2)}, u32[]{:S(2)}) %collective-permute-start.1) | collective-permute-done | bytes 131104 | tf_op jit(solution)/shard_map/ppermute | solution.py:39
  62.6 0.0 collective-permute-done
  62.7 1.9 %collective-permute-start.3 = (f32[128,128]{1,0:T(8,128)S(1)}, f32[128,128]{1,0:T(8,128)S(1)}, u32[]{:S(2)}, u32[]{:S(2)}) collective-permute-start(f32[128,128]{1,0:T(8,128)S(1)} %slice.47), channel_id=1, source_target_pairs={{0,4},{4,0},{8,12},{12,8},{1,5},{5,1},{9,13},{13,9},{2,6},{6,2},{1... | collective-permute-start | bytes 196616 | tf_op jit(solution)/shard_map/ppermute | solution.py:39
  64.6 0.9 collective-permute-done.3
  65.5 5.9 %collective-permute-start.4 = (f32[128,128]{1,0:T(8,128)S(1)}, f32[128,128]{1,0:T(8,128)S(1)}, u32[]{:S(2)}, u32[]{:S(2)}) collective-permute-start(f32[128,128]{1,0:T(8,128)S(1)} %get-tuple-element.18), channel_id=1, source_target_pairs={{0,8},{4,12},{8,0},{12,4},{1,9},{5,13},{9,1},{13,5},{2,10},{6,14},... | collective-permute-start | bytes 196616 | tf_op jit(solution)/shard_map/ppermute | solution.py:39
  71.4 2.2 %collective-permute-done.4 = f32[128,128]{1,0:T(8,128)S(1)} collective-permute-done((f32[128,128]{1,0:T(8,128)S(1)}, f32[128,128]{1,0:T(8,128)S(1)}, u32[]{:S(2)}, u32[]{:S(2)}) %collective-permute-start.4) | collective-permute-done | bytes 65568 | tf_op jit(solution)/shard_map/ppermute | solution.py:39
  73.6 0.0 all-to-all-done.1
  73.6 0.0 copy-start.1
  73.6 1.6 %broadcast_in_dim.33 = f32[16,256,128]{2,1,0:T(8,128)} broadcast(f32[256,128]{1,0:T(8,128)S(1)} %pad_maximum_fusion.3), dimensions={1,2} | broadcast | bytes 2228224 | tf_op jit(solution)/shard_map/broadcast_in_dim | solution.py:85
  75.3 0.0 copy-done.1
  75.3 6.9 %all-to-all-start.2 = ((f32[16,256,128]{2,1,0:T(8,128)}), f32[16,256,128]{2,1,0:T(8,128)}, u32[]{:S(2)}, u32[]{:S(2)}) async-start(f32[16,256,128]{2,1,0:T(8,128)} %broadcast_in_dim.33), calls=%async_computation.2 | async-start | bytes 4194304 | tf_op jit(solution)/shard_map/all_to_all | solution.py:84
  82.2 0.0 copy-done.6
  82.2 0.2 convert_reduce_fusion
  82.4 0.7 compare_reduce_fusion.1
  83.1 0.7 fusion.21
  87.1 21.6 %all-to-all-done.2 = f32[16,256,128]{2,1,0:T(8,128)} async-done(((f32[16,256,128]{2,1,0:T(8,128)}), f32[16,256,128]{2,1,0:T(8,128)}, u32[]{:S(2)}, u32[]{:S(2)}) %all-to-all-start.2) | async-done | bytes 2097184 | tf_op jit(solution)/shard_map/all_to_all | solution.py:84
  108.7 1.7 %fusion.8 = f32[16,128,128]{2,1,0:T(8,128)S(1)} fusion(f32[16,256,128]{2,1,0:T(8,128)} %all-to-all-done.2, f32[16,128,128]{2,1,0:T(8,128)} %param.10), kind=kLoop, calls=%fused_computation.17 | loop fusion | flops 786432 | bytes 3145728 | tf_op jit(solution)/shard_map/add | solution.py:87
  110.4 0.0 copy-start.2
  110.4 0.9 copy-done.2
  111.4 0.2 select_reduce_fusion
  111.6 0.3 abs_reduce_fusion
  111.9 0.1 reduce_max.9
  112.0 0.9 fusion.9
  112.9 0.8 convolution_subtract_fusion.3
  113.7 0.8 fusion.25
  114.6 0.8 convolution_subtract_fusion.2
  115.4 0.8 fusion.24
  116.2 0.8 convolution_subtract_fusion.1
  117.0 0.8 fusion.23
  117.8 0.8 convolution_subtract_fusion
  118.6 1.3 fusion.26
  120.0 0.6 fusion.28
  120.6 0.6 fusion.17
  121.2 0.6 fusion.29
  121.8 0.6 fusion.16
  122.4 0.8 multiply_reduce_fusion
  125.2 14.1 %psum.7 = f32[]{:T(128)} all-reduce(f32[]{:T(128)S(6)} %add.69), channel_id=1, replica_groups=mesh['shards'=16,'tensor'=4,'replica'=4] {'tensor'}, use_global_device_ids=true, to_apply=%region_6.7 | all-reduce | flops 1 | bytes 8 | tf_op jit(solution)/shard_map/psum | solution.py:124
  140.0 2.1 %dynamic-slice_select_fusion.1 = (f32[1,128,128]{2,1,0:T(8,128)S(1)}, f32[1,128,128]{2,1,0:T(8,128)S(1)}) fusion(f32[16,128,128]{2,1,0:T(8,128)} %copy-done.2, s32[]{:T(128)S(6)} %select_n.46, pred[]{:T(512)} %get-tuple-element.7, s32[]{:T(128)S(6)} %select_n.50, pred[]{:T(512)} %get-tuple-element.8), kind=kLoop, calls=%fused_computation.39 | loop fusion | flops 32768 | bytes 262154 | tf_op jit(solution)/shard_map/jit(_where)/select_n | solution.py:106
  142.1 0.7 pad_maximum_fusion.4
  142.8 0.6 multiply_add_fusion.1
  143.4 2.3 %fusion.7 = f32[1024,256]{1,0:T(8,128)} fusion(f32[1024,256]{1,0:T(8,128)} %bitcast.53, f32[1024,128]{1,0:T(8,128)S(1)} %bitcast.52, f32[1024,128]{1,0:T(8,128)S(1)} %bitcast.50, f32[]{:T(128)S(6)} %mul_shard_map.3), kind=kLoop, calls=%fused_computation.15 | loop fusion | flops 786432 | bytes 3145732 | tf_op jit(solution)/shard_map/sub | solution.py:130
  (13 shorter events, 0.2 us)
Async XLA Ops:
  0.6 1.6 %copy-start = (bf16[1024,1024]{1,0:T(8,128)(2,1)S(1)}, bf16[1024,1024]{1,0:T(8,128)(2,1)}, u32[]{:S(2)}) copy-start(bf16[1024,1024]{1,0:T(8,128)(2,1)} %param.7) | copy-start | bytes 6291460
  0.6 2.6 %copy-start.7 = (bf16[1024,1024]{1,0:T(8,128)(2,1)S(1)}, bf16[1024,1024]{1,0:T(8,128)(2,1)}, u32[]{:S(2)}) copy-start(bf16[1024,1024]{1,0:T(8,128)(2,1)} %param.8) | copy-start | bytes 6291460
  3.3 1.2 copy-start.3
  6.1 7.8 %copy-start.4 = (f32[16,256]{1,0:T(8,128)S(1)}, f32[16,256]{1,0:T(8,128)}, u32[]{:S(2)}) copy-start(f32[16,256]{1,0:T(8,128)} %param.13) | copy-start | bytes 49156
  6.1 7.8 %copy-start.5 = (f32[16,256]{1,0:T(8,128)S(1)}, f32[16,256]{1,0:T(8,128)}, u32[]{:S(2)}) copy-start(f32[16,256]{1,0:T(8,128)} %param.12) | copy-start | bytes 49156
  6.1 35.7 %all-to-all-start = ((f32[16,256,128]{2,1,0:T(8,128)}), f32[16,256,128]{2,1,0:T(8,128)}, u32[]{:S(2)}, u32[]{:S(2)}) async-start(f32[16,256,128]{2,1,0:T(8,128)} %pad_maximum_fusion), calls=%async_computation | async-start | bytes 4194304 | tf_op jit(solution)/shard_map/all_to_all | solution.py:77
  42.8 30.8 %all-to-all-start.1 = ((f32[16,64,256]{2,1,0:T(8,128)}), f32[16,64,256]{2,1,0:T(8,128)S(1)}, u32[]{:S(2)}, u32[]{:S(2)}) async-start(f32[16,64,256]{2,1,0:T(8,128)} %stack.4), calls=%async_computation.1 | async-start | bytes 2097152 | tf_op jit(solution)/shard_map/all_to_all | solution.py:64
  48.5 7.1 %collective-permute-start.2 = (f32[256,128]{1,0:T(8,128)S(1)}, f32[256,128]{1,0:T(8,128)S(1)}, u32[]{:S(2)}, u32[]{:S(2)}) collective-permute-start(f32[256,128]{1,0:T(8,128)S(1)} %reduce_sum.73), channel_id=1, source_target_pairs={{0,3},{1,2},{2,1},{3,0},{4,7},{5,6},{6,5},{7,4},{8,11},{9,10},{10,... | collective-permute-start | bytes 393224 | tf_op jit(solution)/shard_map/ppermute | solution.py:39
  52.9 9.7 %collective-permute-start.1 = (f32[256,128]{1,0:T(8,128)S(1)}, f32[256,128]{1,0:T(8,128)S(1)}, u32[]{:S(2)}, u32[]{:S(2)}) collective-permute-start(f32[256,128]{1,0:T(8,128)S(1)} %reduce_sum.73), channel_id=1, source_target_pairs={{0,2},{1,3},{2,0},{3,1},{4,6},{5,7},{6,4},{7,5},{8,10},{9,11},{10,... | collective-permute-start | bytes 393224 | tf_op jit(solution)/shard_map/ppermute | solution.py:39
  52.9 9.7 %collective-permute-start = (f32[256,128]{1,0:T(8,128)S(1)}, f32[256,128]{1,0:T(8,128)S(1)}, u32[]{:S(2)}, u32[]{:S(2)}) collective-permute-start(f32[256,128]{1,0:T(8,128)S(1)} %reduce_sum.73), channel_id=1, source_target_pairs={{0,1},{1,0},{2,3},{3,2},{4,5},{5,4},{6,7},{7,6},{8,9},{9,8},{10,11... | collective-permute-start | bytes 393224 | tf_op jit(solution)/shard_map/ppermute | solution.py:39
  62.7 2.8 %collective-permute-start.3 = (f32[128,128]{1,0:T(8,128)S(1)}, f32[128,128]{1,0:T(8,128)S(1)}, u32[]{:S(2)}, u32[]{:S(2)}) collective-permute-start(f32[128,128]{1,0:T(8,128)S(1)} %slice.47), channel_id=1, source_target_pairs={{0,4},{4,0},{8,12},{12,8},{1,5},{5,1},{9,13},{13,9},{2,6},{6,2},{1... | collective-permute-start | bytes 196616 | tf_op jit(solution)/shard_map/ppermute | solution.py:39
  65.5 8.1 %collective-permute-start.4 = (f32[128,128]{1,0:T(8,128)S(1)}, f32[128,128]{1,0:T(8,128)S(1)}, u32[]{:S(2)}, u32[]{:S(2)}) collective-permute-start(f32[128,128]{1,0:T(8,128)S(1)} %get-tuple-element.18), channel_id=1, source_target_pairs={{0,8},{4,12},{8,0},{12,4},{1,9},{5,13},{9,1},{13,5},{2,10},{6,14},... | collective-permute-start | bytes 196616 | tf_op jit(solution)/shard_map/ppermute | solution.py:39
  73.6 1.6 %copy-start.1 = (f32[16,64,256]{2,1,0:T(8,128)}, f32[16,64,256]{2,1,0:T(8,128)S(1)}, u32[]{:S(2)}) copy-start(f32[16,64,256]{2,1,0:T(8,128)S(1)} %all-to-all-done.1) | copy-start | bytes 3145732
  75.3 6.9 %copy-start.6 = (s32[16]{0:T(128)S(1)}, s32[16]{0:T(128)}, u32[]{:S(2)}) copy-start(s32[16]{0:T(128)} %param.11) | copy-start | bytes 196
  75.3 33.4 %all-to-all-start.2 = ((f32[16,256,128]{2,1,0:T(8,128)}), f32[16,256,128]{2,1,0:T(8,128)}, u32[]{:S(2)}, u32[]{:S(2)}) async-start(f32[16,256,128]{2,1,0:T(8,128)} %broadcast_in_dim.33), calls=%async_computation.2 | async-start | bytes 4194304 | tf_op jit(solution)/shard_map/all_to_all | solution.py:84
  110.4 1.0 copy-start.2
